TPU v7x, 256 devices: a whole 4x4x8 slice. The times are simulated.
256 devices in a mesh: wa: 64 (over z, x, core), gy: 4 (over y).
Axes of the slice: x: 4, y: 4, z: 8, core: 2. Of those that a mesh axis runs over, the one named last changes fastest.
Arguments:
- bricks: bfloat16 [1024, 64, 4096], P('wa', None, 'gy'), may hold values from -6 to 6
- brick_coords: int32 [1024, 2], P('wa'), may hold values from 0 to 15, as said below
- counts: int32 [64], P('wa'), may hold values from 1 to 16, as said below
- green_kernel: bfloat16 [64, 2048, 2048], P('wa', 'gy'), may hold values from 0.19921875 to 4
Outputs:
- potential_hat: bfloat16 [64, 2, 2048, 2048], P('wa', None, 'gy')
Inputs may be any that keep to these rules, and one draw needn't show every extreme that they name: Each owner's occupied slots are its first counts[o] slots; in every draw one owner fills all 16. `brick_coords`: column entries are below 2, z bricks below 16; the pairs of one owner's 16 slots are distinct.
All inputs are finite; a program needn't handle non-finite values.
Results may differ from a plain program's by a relative error of at most 0.0072.
Values may be sent and summed in bfloat16 or wider, within the bound.
A program may use at most 128 MiB of HBM per device.

v0:
```python
import math
import jax
import jax.numpy as jnp
import ml_dtypes
import numpy as np
from jax import lax
from jax.sharding import PartitionSpec as P

BX = 16
BZ = 16
COL_DEV = 2


def wave(positions, frequency, length, factor):
    angles = positions[:, None] * frequency[None, :] % length * (2.0 * math.pi / length)
    return (
        (np.cos(angles) * factor).astype(ml_dtypes.bfloat16),
        (np.sin(angles) * factor).astype(ml_dtypes.bfloat16),
    )


def on_device(bricks, brick_coords, counts, green_kernel):
    depth_count, kx_count, length = green_kernel.shape
    owners = lax.axis_size("wa")
    groups = lax.axis_size("gy")
    depth_total = depth_count * owners
    slot_count, edge, cells = bricks.shape
    rows_brick = cells // edge
    depth_cosine, depth_sine = wave(
        np.arange(BZ * edge), np.arange(depth_total), length, 1.0 / math.sqrt(BZ * edge)
    )
    table = np.concatenate(
        [depth_cosine, (-depth_sine.astype(np.float32)).astype(ml_dtypes.bfloat16)], 1
    )
    table = jnp.asarray(table.reshape(BZ, edge, 2 * depth_total).transpose(0, 2, 1))
    picked = jnp.take(table, brick_coords[:, 1], axis=0)
    alive = jnp.arange(slot_count, dtype=jnp.int32) < counts[0]
    mine = (brick_coords[:, 0][None, :] == jnp.arange(COL_DEV, dtype=jnp.int32)[:, None]) & alive[
        None, :
    ]
    mixing = picked[None] * mine[:, :, None, None].astype(jnp.bfloat16)
    sums = jnp.einsum("gsqz,szc->gqc", mixing, bricks, preferred_element_type=jnp.float32)
    spectra = sums.astype(jnp.bfloat16).reshape(COL_DEV, 2, depth_total, rows_brick, edge)
    spectra = spectra.transpose(2, 1, 3, 0, 4).reshape(depth_total, 2, rows_brick, COL_DEV * edge)
    arrived = lax.all_to_all(spectra, "wa", split_axis=0, concat_axis=0, tiled=True)
    wide = BX // COL_DEV
    brick_rows = owners // wide
    local_rows = brick_rows * rows_brick
    layout = arrived.reshape(brick_rows, wide, 2, rows_brick, COL_DEV * edge)
    layout = layout.transpose(2, 0, 3, 1, 4).reshape(2, local_rows, BX * edge)
    cosine, sine = wave(np.arange(BX * edge), np.arange(length), length, 1.0 / math.sqrt(BX * edge))
    negative = (-sine.astype(np.float32)).astype(ml_dtypes.bfloat16)
    both = jnp.asarray(np.stack([np.stack([cosine, sine]), np.stack([negative, cosine])], 0))
    planes = jnp.einsum("pyx,opxq->oyq", layout, both, preferred_element_type=jnp.float32).astype(
        jnp.bfloat16
    )
    regrouped = lax.all_to_all(planes, "gy", split_axis=2, concat_axis=1, tiled=True)
    every = np.arange(groups * local_rows)
    source, within = (every // local_rows, every % local_rows)
    global_rows = within // rows_brick * edge + source * rows_brick + within % rows_brick
    cosine, sine = wave(global_rows, np.arange(length), length, 1.0 / math.sqrt(brick_rows * edge))
    negative = (-sine.astype(np.float32)).astype(ml_dtypes.bfloat16)
    both = jnp.asarray(np.stack([np.stack([cosine, sine]), np.stack([negative, cosine])], 0))
    final = jnp.einsum("pyx,opyr->oxr", regrouped, both, preferred_element_type=jnp.float32)
    return (final * green_kernel.astype(jnp.float32)).astype(jnp.bfloat16)[None]


def solution(mesh):
    return jax.shard_map(
        on_device,
        mesh=mesh,
        in_specs=(P("wa", None, "gy"), P("wa", None), P("wa"), P("wa", "gy", None)),
        out_specs=P("wa", None, "gy", None),
        check_vma=False,
    )
```

profile of v0, /device:TPU:1, one launch (start us, length us, event | category | flops | bytes accessed | tf_op | source)
XLA Modules:
  0.0 86.4 jit_solution(8450380916489983388)
XLA Ops:
  0.0 0.0 copy-start
  0.0 0.8 and_bitcast_fusion
  0.8 0.8 fusion.15
  2.3 1.5 %gather_fusion = bf16[16,128,64]{1,2,0:T(8,128)(2,1)S(1)} fusion(bf16[16,128,64]{1,2,0:T(8,128)(2,1)} %constant.22.clone, s32[1024]{0:T(1024)S(1)} %pad_clamp_fusion), kind=kCustom, calls=%fused_computation | custom fusion | bytes 524352 | tf_op jit(solution)/shard_map/jit(_take)/gather | solution.py:36
  3.8 0.1 broadcast_select_fusion
  3.9 0.0 copy-done
  4.0 1.6 %fusion.9 = bf16[2,128,1024]{2,1,0:T(8,128)(2,1)} fusion(bf16[16,64,1024]{2,1,0:T(8,128)(2,1)S(1)} %copy-done, bf16[2,16]{1,0:T(2,128)(2,1)S(1)} %and_convert_fusion, bf16[16,128,64]{1,2,0:T(8,128)(2,1)S(1)} %broadcast_select_fusion), kind=kOutput, calls=%fused_computation.11 | convolution fusion | flops 537395200 | bytes 2883648 | tf_op jit(solution)/shard_map/gsqz,szc->gqc/dot_general | solution.py:42
  5.6 1.8 %reshape.58 = bf16[2,2,64,16,64]{4,3,2,1,0:T(8,128)(2,1)S(1)} reshape(bf16[2,128,1024]{2,1,0:T(8,128)(2,1)} %fusion.9) | data formatting | bytes 1048576 | tf_op jit(solution)/shard_map/reshape | solution.py:43
  7.3 2.6 %copy.22 = bf16[2,2,64,16,64]{4,0,3,1,2:T(2,128)(2,1)} copy(bf16[2,2,64,16,64]{4,3,2,1,0:T(8,128)(2,1)S(1)} %reshape.58) | data formatting | bytes 1048576 | tf_op jit(solution)/shard_map/reshape | solution.py:43
  9.9 2.4 %reshape.59 = bf16[64,2,16,128]{3,2,1,0:T(8,128)(2,1)S(1)} reshape(bf16[64,2,16,2,64]{4,3,2,1,0:T(2,128)(2,1)} %bitcast.62) | data formatting | bytes 1048576 | tf_op jit(solution)/shard_map/reshape | solution.py:44
  12.3 30.5 %all_to_all.23 = bf16[64,2,16,128]{3,2,1,0:T(8,128)(2,1)S(1)} all-to-all(bf16[64,2,16,128]{3,2,1,0:T(8,128)(2,1)S(1)} %reshape.59), channel_id=1, replica_groups=mesh['wa'=64,'gy'=4] {'wa'}, dimensions={0} | all-to-all | bytes 1048576 | tf_op jit(solution)/shard_map/all_to_all | solution.py:45
  42.8 0.2 copy.13
  43.0 1.0 %reshape.73 = bf16[2,128,1024,1]{2,1,0,3:T(8,128)(2,1)} reshape(bf16[2,8,16,8,128]{4,3,2,1,0:T(8,128)(2,1)S(1)} %copy.13) | data formatting | bytes 1048576 | tf_op jit(solution)/shard_map/reshape | solution.py:50
  44.1 8.3 %fusion.3 = bf16[2,128,2048]{2,1,0:T(8,128)(2,1)S(1)} fusion(bf16[2,128,1024,1]{2,1,0,3:T(8,128)(2,1)} %reshape.73, bf16[2,2,1024,2048]{3,2,1,0:T(8,128)(2,1)} %constant.23.clone), kind=kOutput, calls=%fused_computation.6 | convolution fusion | flops 2148007936 | bytes 18350080 | tf_op jit(solution)/shard_map/pyx,opxq->oyq/dot_general | solution.py:54
  52.4 2.0 %copy.14 = bf16[2,128,2048]{1,0,2:T(2,128)(2,1)} copy(bf16[2,128,2048]{2,1,0:T(8,128)(2,1)S(1)} %fusion.3) | data formatting | bytes 2097152 | tf_op jit(solution)/shard_map/convert_element_type | solution.py:54
  54.4 4.2 %all-to-all-start.1 = ((bf16[2,128,2048]{1,0,2:T(2,128)(2,1)}), bf16[2,128,2048]{1,0,2:T(2,128)(2,1)S(1)}, u32[]{:S(2)}, u32[]{:S(2)}) async-start(bf16[2,128,2048]{1,0,2:T(2,128)(2,1)} %copy.14), calls=%async_computation.1 | async-start | bytes 2097152 | tf_op jit(solution)/shard_map/all_to_all | solution.py:57
  58.5 4.1 %bitcast_convert_fusion = f32[512,2048]{1,0:T(8,128)} fusion(bf16[1,512,2048]{2,1,0:T(8,128)(2,1)} %param.10), kind=kLoop, calls=%fused_computation.7 | loop fusion | flops 1048576 | bytes 6291456 | tf_op jit(solution)/shard_map/mul | solution.py:65
  62.6 10.4 %all-to-all-done.1 = bf16[2,128,2048]{1,0,2:T(2,128)(2,1)S(1)} async-done(((bf16[2,128,2048]{1,0,2:T(2,128)(2,1)}), bf16[2,128,2048]{1,0,2:T(2,128)(2,1)S(1)}, u32[]{:S(2)}, u32[]{:S(2)}) %all-to-all-start.1) | async-done | bytes 1048608 | tf_op jit(solution)/shard_map/all_to_all | solution.py:57
  73.0 1.8 %copy.21 = bf16[2,128,4,512]{1,2,3,0:T(4,128)(2,1)} copy(bf16[2,128,4,512]{1,0,3,2:T(2,128)(2,1)S(1)} %bitcast.61) | data formatting | bytes 2097152 | tf_op jit(solution)/shard_map/all_to_all | solution.py:57
  74.8 1.5 %reshape.75 = bf16[2,512,512,1]{1,2,0,3:T(8,128)(2,1)S(1)} reshape(bf16[2,4,128,512]{2,1,3,0:T(4,128)(2,1)} %bitcast.63) | data formatting | bytes 2097152 | tf_op jit(solution)/shard_map/all_to_all | solution.py:57
  76.3 10.1 %fusion.1 = bf16[1,2,512,2048]{3,2,1,0:T(8,128)(2,1)} fusion(f32[512,2048]{1,0:T(8,128)} %bitcast_convert_fusion, bf16[2,512,512,1]{1,2,0,3:T(8,128)(2,1)S(1)} %reshape.75, bf16[2,2,512,2048]{3,2,1,0:T(8,128)(2,1)} %constant.24.clone), kind=kOutput, calls=%fused_computation.3 | convolution fusion | flops 4299161600 | bytes 17825792 | tf_op jit(solution)/shard_map/pyx,opyr->oxr/dot_general | solution.py:64
  (3 shorter events, 0.0 us)
Async XLA Ops:
  0.0 3.9 %copy-start = (bf16[16,64,1024]{2,1,0:T(8,128)(2,1)S(1)}, bf16[16,64,1024]{2,1,0:T(8,128)(2,1)}, u32[]{:S(2)}) copy-start(bf16[16,64,1024]{2,1,0:T(8,128)(2,1)} %param.7) | copy-start | bytes 6291460
  54.4 18.7 %all-to-all-start.1 = ((bf16[2,128,2048]{1,0,2:T(2,128)(2,1)}), bf16[2,128,2048]{1,0,2:T(2,128)(2,1)S(1)}, u32[]{:S(2)}, u32[]{:S(2)}) async-start(bf16[2,128,2048]{1,0,2:T(2,128)(2,1)} %copy.14), calls=%async_computation.1 | async-start | bytes 2097152 | tf_op jit(solution)/shard_map/all_to_all | solution.py:57
where the time goes:
time: 86.7 us; the launch traced here: 86.4 us
  blocking collectives  30.5 us (35%)
  matrix products  20 us (23%)
  local copies, waits for them, and re-layouts  14.8 us (17%)
  waiting for transfers between devices  10.4 us (12%)
  other arithmetic  5.76 us (7%)
  starting transfers between devices  4.18 us (5%)
    all_to_all x1, blocking collectives, on_device(): lax.all_to_all(spectra, 'wa', split_axis=0, concat_axis=0, tiled=True)  30.5 us
    all_to_all x1, waiting for transfers between devices, on_device(): lax.all_to_all(planes, 'gy', split_axis=2, concat_axis=1, tiled=True)  10.4 us
    dot_general x1, matrix products, on_device(): jnp.einsum('pyx,opyr->oxr', regrouped, both, preferred_element_type=jnp.f...  10.1 us
    dot_general x1, matrix products, on_device(): jnp.einsum('pyx,opxq->oyq', layout, both, preferred_element_type=jnp.floa...  8.29 us
    reshape x2, local copies, waits for them, and re-layouts, on_device(): sums.astype(jnp.bfloat16).reshape(COL_DEV, 2, depth_total, rows_brick, edge)  4.34 us
    all_to_all x1, starting transfers between devices, on_device(): lax.all_to_all(planes, 'gy', split_axis=2, concat_axis=1, tiled=True)  4.18 us
    mul x1, other arithmetic, on_device(): return (final * green_kernel.astype(jnp.float32)).astype(jnp.bfloat16)[None]  4.06 us
    all_to_all x2, local copies, waits for them, and re-layouts, on_device(): lax.all_to_all(planes, 'gy', split_axis=2, concat_axis=1, tiled=True)  3.25 us
  transfers between devices with their start and end apart: 1, of which 1 were waited for; matrix products, arithmetic and copies ran while one was open for 5% of the time, Pallas kernels for 0%

commit v1 on v0

--- a/solution.py
+++ b/solution.py
@@ -54,7 +54,15 @@
     planes = jnp.einsum("pyx,opxq->oyq", layout, both, preferred_element_type=jnp.float32).astype(
         jnp.bfloat16
     )
-    regrouped = lax.all_to_all(planes, "gy", split_axis=2, concat_axis=1, tiled=True)
+    regrouped = jnp.concatenate(
+        lax.all_to_all(
+            jnp.stack(jnp.split(planes, lax.axis_size("gy"), 2), 0),
+            axis_name="gy",
+            concat_axis=0,
+            split_axis=0,
+        ),
+        1,
+    )
     every = np.arange(groups * local_rows)
     source, within = (every // local_rows, every % local_rows)
     global_rows = within // rows_brick * edge + source * rows_brick + within % rows_brick

time: 86.7 us -> 82 us (0.946)
  local copies, waits for them, and re-layouts: 14.8 us -> 8.9 us
  other arithmetic: 5.76 us -> 6.86 us
    all_to_all x2 -> x0, local copies, waits for them, and re-layouts: 3.25 us -> none  [on_device(): lax.all_to_all(planes, 'gy', split_axis=2, concat_axis=1, tiled=True)]
    convert_element_type x1 -> x0, local copies, waits for them, and re-layouts: 2 us -> none  [on_device(): jnp.einsum('pyx,opxq->oyq', layout, both, preferred_element_type=jnp.floa...]
    another operation x0 -> x1, other arithmetic: none -> 1.1 us  [on_device(): jnp.stack(jnp.split(planes, lax.axis_size('gy'), 2), 0)]
where the time goes in v1:
time: 82 us; the launch traced here: 81.6 us
  blocking collectives  30.5 us (37%)
  matrix products  20 us (24%)
  waiting for transfers between devices  10.5 us (13%)
  local copies, waits for them, and re-layouts  8.9 us (11%)
  other arithmetic  6.86 us (8%)
  starting transfers between devices  4.18 us (5%)
    all_to_all x1, blocking collectives, on_device(): lax.all_to_all(spectra, 'wa', split_axis=0, concat_axis=0, tiled=True)  30.5 us
    all_to_all x1, waiting for transfers between devices, on_device(): lax.all_to_all(jnp.stack(jnp.split(planes, lax.axis_size('gy'), 2), 0), a...  10.5 us
    dot_general x1, matrix products, on_device(): jnp.einsum('pyx,opyr->oxr', regrouped, both, preferred_element_type=jnp.f...  10.2 us
    dot_general x1, matrix products, on_device(): jnp.einsum('pyx,opxq->oyq', layout, both, preferred_element_type=jnp.floa...  8.12 us
    reshape x2, local copies, waits for them, and re-layouts, on_device(): sums.astype(jnp.bfloat16).reshape(COL_DEV, 2, depth_total, rows_brick, edge)  4.34 us
    all_to_all x1, starting transfers between devices, on_device(): lax.all_to_all(jnp.stack(jnp.split(planes, lax.axis_size('gy'), 2), 0), a...  4.18 us
    mul x1, other arithmetic, on_device(): return (final * green_kernel.astype(jnp.float32)).astype(jnp.bfloat16)[None]  4.05 us
    reshape x1, local copies, waits for them, and re-layouts, on_device(): spectra.transpose(2, 1, 3, 0, 4)  2.41 us
  transfers between devices with their start and end apart: 1, of which 1 were waited for; matrix products, arithmetic and copies ran while one was open for 5% of the time, Pallas kernels for 0%

profile of v1, /device:TPU:1, one launch (start us, length us, event | category | flops | bytes accessed | tf_op | source)
XLA Modules:
  0.0 81.6 jit_solution(11149261689291990993)
XLA Ops:
  0.0 0.0 copy-start
  0.0 0.8 %and_bitcast_fusion = pred[16]{0:T(512)(128)(4,1)S(1)} fusion(s32[16,2]{0,1:T(2,128)} %param.8), kind=kLoop, calls=%fused_computation.25 | loop fusion | flops 96 | bytes 80 | tf_op jit(solution)/shard_map/jit(_take)/reduce_and | solution.py:36
  0.8 0.8 fusion.15
  2.3 1.5 %gather_fusion = bf16[16,128,64]{1,2,0:T(8,128)(2,1)S(1)} fusion(bf16[16,128,64]{1,2,0:T(8,128)(2,1)} %constant.22.clone, s32[1024]{0:T(1024)S(1)} %pad_clamp_fusion), kind=kCustom, calls=%fused_computation | custom fusion | bytes 524352 | tf_op jit(solution)/shard_map/jit(_take)/gather | solution.py:36
  3.8 0.1 broadcast_select_fusion
  3.9 0.0 copy-done
  4.0 1.6 %fusion.9 = bf16[2,128,1024]{2,1,0:T(8,128)(2,1)} fusion(bf16[16,64,1024]{2,1,0:T(8,128)(2,1)S(1)} %copy-done, bf16[2,16]{1,0:T(2,128)(2,1)S(1)} %and_convert_fusion, bf16[16,128,64]{1,2,0:T(8,128)(2,1)S(1)} %broadcast_select_fusion), kind=kOutput, calls=%fused_computation.11 | convolution fusion | flops 537395200 | bytes 2883648 | tf_op jit(solution)/shard_map/gsqz,szc->gqc/dot_general | solution.py:42
  5.6 1.8 %reshape.64 = bf16[2,2,64,16,64]{4,3,2,1,0:T(8,128)(2,1)S(1)} reshape(bf16[2,128,1024]{2,1,0:T(8,128)(2,1)} %fusion.9) | data formatting | bytes 1048576 | tf_op jit(solution)/shard_map/reshape | solution.py:43
  7.3 2.6 %copy.18 = bf16[2,2,64,16,64]{4,0,3,1,2:T(2,128)(2,1)} copy(bf16[2,2,64,16,64]{4,3,2,1,0:T(8,128)(2,1)S(1)} %reshape.64) | data formatting | bytes 1048576 | tf_op jit(solution)/shard_map/reshape | solution.py:43
  9.9 2.4 %reshape.65 = bf16[64,2,16,128]{3,2,1,0:T(8,128)(2,1)S(1)} reshape(bf16[64,2,16,2,64]{4,3,2,1,0:T(2,128)(2,1)} %bitcast.68) | data formatting | bytes 1048576 | tf_op jit(solution)/shard_map/reshape | solution.py:44
  12.3 30.5 %all_to_all.10 = bf16[64,2,16,128]{3,2,1,0:T(8,128)(2,1)S(1)} all-to-all(bf16[64,2,16,128]{3,2,1,0:T(8,128)(2,1)S(1)} %reshape.65), channel_id=1, replica_groups=mesh['wa'=64,'gy'=4] {'wa'}, dimensions={0} | all-to-all | bytes 1048576 | tf_op jit(solution)/shard_map/all_to_all | solution.py:45
  42.8 0.2 copy.9
  43.0 0.2 reshape.81
  43.3 8.1 %fusion.3 = bf16[2,128,2048]{2,1,0:T(8,128)(2,1)S(1)} fusion(bf16[2,128,1024,1]{2,1,0,3:T(8,128)(2,1)S(1)} %reshape.81, bf16[2,2,1024,2048]{3,2,1,0:T(8,128)(2,1)} %constant.23.clone), kind=kOutput, calls=%fused_computation.6 | convolution fusion | flops 2148007936 | bytes 18350080 | tf_op jit(solution)/shard_map/pyx,opxq->oyq/dot_general | solution.py:54
  51.4 0.1 slice_bitcast_fusion.3
  51.5 1.1 %pad_maximum_fusion = bf16[4,2,128,512]{3,2,1,0:T(8,128)(2,1)} fusion(bf16[1,2,128,512]{3,2,1,0:T(8,128)(2,1)S(1)} %get-tuple-element.6, bf16[1,2,128,512]{3,2,1,0:T(8,128)(2,1)S(1)} %get-tuple-element.7, bf16[1,2,128,512]{3,2,1,0:T(8,128)(2,1)S(1)} %get-tuple-element.8, bf16[1,2,128,512]{3,2,1,0:T(8,128)(2,1)S(1)} %get-tuple-element.5), kind=kLoop, calls=%fused_computation.12 | loop fusion | flops 1572864 | bytes 2097152 | tf_op jit(solution)/shard_map/stack | solution.py:59
  52.6 4.2 %all-to-all-start.1 = ((bf16[4,2,128,512]{3,2,1,0:T(8,128)(2,1)}), bf16[4,2,128,512]{3,2,1,0:T(8,128)(2,1)S(1)}, u32[]{:S(2)}, u32[]{:S(2)}) async-start(bf16[4,2,128,512]{3,2,1,0:T(8,128)(2,1)} %pad_maximum_fusion), calls=%async_computation.1 | async-start | bytes 2097152 | tf_op jit(solution)/shard_map/all_to_all | solution.py:58
  56.8 4.1 %bitcast_convert_fusion = f32[512,2048]{1,0:T(8,128)} fusion(bf16[1,512,2048]{2,1,0:T(8,128)(2,1)} %param.10), kind=kLoop, calls=%fused_computation.7 | loop fusion | flops 1048576 | bytes 6291456 | tf_op jit(solution)/shard_map/mul | solution.py:73
  60.8 10.5 %all-to-all-done.1 = bf16[4,2,128,512]{3,2,1,0:T(8,128)(2,1)S(1)} async-done(((bf16[4,2,128,512]{3,2,1,0:T(8,128)(2,1)}), bf16[4,2,128,512]{3,2,1,0:T(8,128)(2,1)S(1)}, u32[]{:S(2)}, u32[]{:S(2)}) %all-to-all-start.1) | async-done | bytes 1048608 | tf_op jit(solution)/shard_map/all_to_all | solution.py:58
  71.3 0.1 copy.10
  71.4 10.2 %fusion.1 = bf16[1,2,512,2048]{3,2,1,0:T(8,128)(2,1)} fusion(f32[512,2048]{1,0:T(8,128)} %bitcast_convert_fusion, bf16[2,512,512,1]{2,1,0,3:T(8,128)(2,1)S(1)} %bitcast.70, bf16[2,2,512,2048]{3,2,1,0:T(8,128)(2,1)} %constant.24.clone), kind=kOutput, calls=%fused_computation.3 | convolution fusion | flops 4299161600 | bytes 17825792 | tf_op jit(solution)/shard_map/pyx,opyr->oxr/dot_general | solution.py:72
  (3 shorter events, 0.0 us)
Async XLA Ops:
  0.0 3.9 %copy-start = (bf16[16,64,1024]{2,1,0:T(8,128)(2,1)S(1)}, bf16[16,64,1024]{2,1,0:T(8,128)(2,1)}, u32[]{:S(2)}) copy-start(bf16[16,64,1024]{2,1,0:T(8,128)(2,1)} %param.7) | copy-start | bytes 6291460
  52.6 18.7 %all-to-all-start.1 = ((bf16[4,2,128,512]{3,2,1,0:T(8,128)(2,1)}), bf16[4,2,128,512]{3,2,1,0:T(8,128)(2,1)S(1)}, u32[]{:S(2)}, u32[]{:S(2)}) async-start(bf16[4,2,128,512]{3,2,1,0:T(8,128)(2,1)} %pad_maximum_fusion), calls=%async_computation.1 | async-start | bytes 2097152 | tf_op jit(solution)/shard_map/all_to_all | solution.py:58
